TPU v7x, 256 devices: a whole 4x4x8 slice. The times are simulated.
256 devices in a mesh: src: 64 (over z_hi, x, y, core), rcv: 4 (over z_lo).
Axes of the slice: x: 4, y: 4, z: 8 (z_hi: 2, z_lo: 4; z = z_hi * 4 + z_lo), core: 2. Of those that a mesh axis runs over, the one named last changes fastest.
Arguments:
- src_spec: bfloat16 [2, 16, 256, 4096], P(None, None, 'rcv', 'src'), may hold values from -6 to 6
- rcv_spec: bfloat16 [2, 16, 256, 1024], P(None, None, 'src', 'rcv'), may hold values from -6 to 6
- lag_table: int32 [16, 8192], replicated, may hold values from 0 to 511
- src_pos: int32 [4096], P('src'), may hold values from 0 to 8191
- rcv_pos: int32 [1024], P('rcv'), may hold values from 0 to 8191
Outputs:
- panel_src: float32 [16, 2, 4096, 256], P(None, None, ('src', 'rcv'))
- panel_rcv: float32 [16, 2, 256, 1024], P(None, None, 'src', 'rcv')
All inputs are finite; a program needn't handle non-finite values.
Results may differ from a plain program's by a relative error of at most 0.0035.
Values may be sent and summed in bfloat16 or wider, within the bound.
A program may use at most 64 MiB of HBM per device.

v0:
```python
import math

import jax
import jax.numpy as jnp
from jax import lax
from jax.sharding import PartitionSpec as P

WIN = 8
SEGS = 2


def phase_table(freqs, lags, n_freq):
    index_mod = freqs[:, None, None] * jnp.transpose(lags)[None, :, :] % (2 * n_freq)
    angles = index_mod.astype(jnp.float32) * (math.pi / n_freq)
    return (jnp.cos(angles), jnp.sin(angles))


def cross_block(src_block, rcv_block):
    block_width = src_block.shape[2]
    src_five = src_block.reshape(2, SEGS, WIN, block_width, src_block.shape[3])
    rcv_five = rcv_block.reshape(2, SEGS, WIN, block_width, rcv_block.shape[3])
    swapped = jnp.stack([src_five[1], -src_five[0]])
    real_part = jnp.einsum(
        "cgwfs,cgwfr->gfsr", src_five, rcv_five, preferred_element_type=jnp.float32
    )
    imag_part = jnp.einsum(
        "cgwfs,cgwfr->gfsr", swapped, rcv_five, preferred_element_type=jnp.float32
    )
    floor_mod = jnp.maximum(jnp.sqrt(real_part * real_part + imag_part * imag_part), 1.0)
    stacked_re = (jnp.sum(real_part / floor_mod, axis=0) / SEGS).astype(jnp.bfloat16)
    stacked_im = (jnp.sum(imag_part / floor_mod, axis=0) / SEGS).astype(jnp.bfloat16)
    return (stacked_re, stacked_im)


def source_slant(stacked_re, stacked_im, rcv_cos, rcv_sin, src_cos, src_sin, factor):
    left_op = jnp.concatenate([stacked_re, stacked_im], axis=2)
    cos_b = rcv_cos.astype(jnp.bfloat16)
    sin_b = rcv_sin.astype(jnp.bfloat16)
    upper_half = jnp.concatenate([cos_b, sin_b], axis=2)
    bottom = jnp.concatenate([-sin_b, cos_b], axis=2)
    right_op = jnp.concatenate([upper_half, bottom], axis=1)
    sums = jnp.einsum("fsk,fkq->fsq", left_op, right_op, preferred_element_type=jnp.float32)
    n_slow = rcv_cos.shape[2]
    sum_re = sums[:, :, :n_slow]
    sum_im = sums[:, :, n_slow:]
    panel_re = (sum_re * src_cos + sum_im * src_sin) * factor
    panel_im = (sum_im * src_cos - sum_re * src_sin) * factor
    return jnp.transpose(jnp.stack([panel_re, panel_im]), (3, 0, 2, 1))


def receiver_right(src_cos_b, src_sin_b):
    upper_half = jnp.concatenate([src_cos_b, -src_sin_b], axis=2)
    bottom = jnp.concatenate([src_sin_b, src_cos_b], axis=2)
    return jnp.concatenate([upper_half, bottom], axis=1)


def receiver_sums(left_op, right_op):
    return jnp.einsum("fkr,fkq->fqr", left_op, right_op, preferred_element_type=jnp.float32)


def receiver_outer(sums, rcv_cos, rcv_sin, factor):
    n_slow = rcv_cos.shape[2]
    cos_t = jnp.transpose(rcv_cos, (0, 2, 1))
    sin_t = jnp.transpose(rcv_sin, (0, 2, 1))
    sum_re = sums[:, :n_slow, :]
    sum_im = sums[:, n_slow:, :]
    panel_re = (sum_re * cos_t - sum_im * sin_t) * factor
    panel_im = (sum_re * sin_t + sum_im * cos_t) * factor
    return jnp.transpose(jnp.stack([panel_re, panel_im]), (2, 0, 1, 3))


def per_device(src_spec, rcv_spec, lag_table, src_pos, rcv_pos):
    src_full = lax.all_gather(src_spec, "rcv", axis=2, tiled=True)
    n_freq = src_full.shape[2]
    src_dev = src_full.shape[3]
    rcv_dev = rcv_spec.shape[3]
    n_slow = lag_table.shape[0]
    n_src = lax.axis_size("src")
    n_rcv = lax.axis_size("rcv")
    src_factor = 1.0 / math.sqrt(rcv_dev * n_rcv)
    rcv_factor = 1.0 / math.sqrt(src_dev * n_src)
    lag_src = jnp.take(lag_table, src_pos, axis=1)
    lag_rcv = jnp.take(lag_table, rcv_pos, axis=1)
    src_init = jnp.zeros((n_slow, 2, src_dev, n_freq), jnp.float32)
    other_init = jnp.zeros((n_slow, 2, n_freq, rcv_dev), jnp.float32)
    shard_piece = lax.all_gather(rcv_spec, "src", axis=2, tiled=True)
    block_width = math.gcd(shard_piece.shape[2], 16)

    def inner(turn_index, totals):
        offset = turn_index * block_width
        freqs = offset + jnp.arange(block_width, dtype=jnp.int32)
        src_block = lax.dynamic_slice_in_dim(src_full, offset, block_width, 2)
        rcv_block = lax.dynamic_slice_in_dim(shard_piece, offset, block_width, 2)
        stacked_re, stacked_im = cross_block(src_block, rcv_block)
        rcv_cos, rcv_sin = phase_table(freqs, lag_rcv, n_freq)
        src_cos, src_sin = phase_table(freqs, lag_src, n_freq)
        src_part = source_slant(
            stacked_re, stacked_im, rcv_cos, rcv_sin, src_cos, src_sin, src_factor
        )
        src_total = lax.dynamic_update_slice_in_dim(totals[0], src_part, offset, 3)
        left_op = jnp.concatenate([stacked_re, stacked_im], axis=1)
        right_op = receiver_right(src_cos.astype(jnp.bfloat16), src_sin.astype(jnp.bfloat16))
        rcv_part = receiver_outer(receiver_sums(left_op, right_op), rcv_cos, rcv_sin, rcv_factor)
        other = lax.dynamic_update_slice_in_dim(totals[1], rcv_part, offset, 2)
        return (src_total, other)

    src_total, other = lax.fori_loop(
        0, shard_piece.shape[2] // block_width, inner, (src_init, other_init)
    )
    panel_src = lax.psum_scatter(src_total, "rcv", scatter_dimension=2, tiled=True)
    panel_rcv = lax.psum_scatter(other, "src", scatter_dimension=2, tiled=True)
    return (panel_src, panel_rcv)


def solution(mesh):
    placed = (P(None, None, "rcv", "src"), P(None, None, "src", "rcv"), P(), P("src"), P("rcv"))
    return jax.shard_map(
        per_device,
        mesh=mesh,
        in_specs=placed,
        out_specs=(P(None, None, ("src", "rcv"), None), P(None, None, "src", "rcv")),
        check_vma=False,
    )
```

profile of v0, /device:TPU:1, one launch (start us, length us, event | category | flops | bytes accessed | tf_op | source)
XLA Modules:
  0.0 853.7 jit_solution(8564354730002031349)
XLA Ops:
  8.0 1.5 copy.29
  9.5 3.5 copy.30
  13.0 2.8 gather_fusion.1
  15.9 2.9 gather_fusion
  19.1 44.0 %all-gather.3.cloned.1.call-done = bf16[2,16,256,64]{3,2,1,0:T(8,128)(2,1)} async-done(((bf16[2,16,64,64]{3,2,1,0:T(8,128)(2,1)}), bf16[2,16,256,64]{3,2,1,0:T(8,128)(2,1)}) %all-gather.3.cloned.1.call-update) | async-done | bytes 1048592 | tf_op jit(solution)/shard_map/all_gather | solution.py:73
  63.1 97.3 %all-gather.5.cloned.1.call-done = bf16[2,16,256,256]{3,1,0,2:T(8,128)(2,1)} async-done(((bf16[2,16,4,256]{3,1,0,2:T(8,128)(2,1)}), bf16[2,16,256,256]{3,1,0,2:T(8,128)(2,1)}) %all-gather.5.cloned.1.call-update) | async-done | bytes 4194320 | tf_op jit(solution)/shard_map/all_gather | solution.py:86
  160.4 2.2 broadcast_in_dim.40
  162.6 4.3 broadcast_in_dim.41.clone
  166.9 212.6 %while.17 = (s32[]{:T(128)}, f32[16,2,64,256]{2,0,3,1:T(8,128)}, f32[16,2,256,256]{3,0,1,2:T(8,128)}, bf16[2,16,256,64]{3,2,1,0:T(8,128)(2,1)}, bf16[2,16,256,25...) while((s32[]{:T(128)}, f32[16,2,64,256]{2,0,3,1:T(8,128)}, ...), condition=%wide.region_3.4_spmd, body=%wide.region_0.3_spmd.sunk | while | flops 116801552 | bytes 17031760 | solution.py:107
  170.5 1.3 sine_convert_fusion.2
  171.7 1.4 fusion.76
  173.2 2.5 fusion.77
  177.4 1.3 multiply_bitcast_fusion.5
  185.0 1.4 fusion.76
  186.5 2.5 fusion.77
  190.7 1.3 multiply_bitcast_fusion.5
  198.3 1.4 fusion.76
  199.8 2.5 fusion.77
  203.9 1.3 multiply_bitcast_fusion.5
  211.6 1.4 fusion.76
  213.1 2.5 fusion.77
  217.2 1.3 multiply_bitcast_fusion.5
  223.7 1.3 sine_convert_fusion.2
  224.9 1.4 fusion.76
  226.4 2.5 fusion.77
  230.5 1.3 multiply_bitcast_fusion.5
  238.2 1.4 fusion.76
  239.6 2.5 fusion.77
  243.8 1.3 multiply_bitcast_fusion.5
  251.5 1.4 fusion.76
  252.9 2.5 fusion.77
  257.1 1.3 multiply_bitcast_fusion.5
  264.8 1.4 fusion.76
  266.2 2.5 fusion.77
  270.4 1.3 multiply_bitcast_fusion.5
  278.1 1.4 fusion.76
  279.5 2.5 fusion.77
  283.7 1.3 multiply_bitcast_fusion.5
  291.4 1.4 fusion.76
  292.8 2.5 fusion.77
  297.0 1.3 multiply_bitcast_fusion.5
  304.6 1.4 fusion.76
  306.1 2.5 fusion.77
  310.2 1.3 multiply_bitcast_fusion.5
  317.9 1.4 fusion.76
  319.4 2.5 fusion.77
  323.5 1.3 multiply_bitcast_fusion.5
  331.2 1.4 fusion.76
  332.6 2.5 fusion.77
  336.8 1.3 multiply_bitcast_fusion.5
  343.2 1.3 sine_convert_fusion.2
  344.5 1.4 fusion.76
  345.9 2.5 fusion.77
  350.1 1.3 multiply_bitcast_fusion.5
  357.8 1.4 fusion.76
  359.2 2.5 fusion.77
  363.4 1.3 multiply_bitcast_fusion.5
  371.1 1.4 fusion.76
  372.5 2.5 fusion.77
  376.7 1.3 multiply_bitcast_fusion.5
  379.6 3.8 copy.35
  383.5 410.5 %reduce-scatter.5.cloned.1.call-done = f32[16,2,4,256]{3,0,1,2:T(8,128)} async-done(((f32[16,2,256,256]{3,0,1,2:T(8,128)}), f32[16,2,4,256]{3,0,1,2:T(8,128)}) %reduce-scatter.5.cloned.1.call-update) | async-done | bytes 131088 | tf_op jit(solution)/shard_map/reduce_scatter | solution.py:111
  794.0 1.6 copy.37
  795.6 51.6 %reduce-scatter.3.cloned.1.call-done = f32[16,2,16,256]{3,2,1,0:T(8,128)} async-done(((f32[16,2,64,256]{3,2,1,0:T(8,128)}), f32[16,2,16,256]{3,2,1,0:T(8,128)}) %reduce-scatter.3.cloned.1.call-update) | async-done | bytes 524304 | tf_op jit(solution)/shard_map/reduce_scatter | solution.py:110
  (243 shorter events, 125.1 us)
Async XLA Ops:
  7.2 5.9 copy-start.1
  7.2 8.7 %copy-start = (s32[256]{0:T(256)S(1)}, s32[256]{0:T(256)}, u32[]{:S(2)}) copy-start(s32[256]{0:T(256)} %param.11) | copy-start | bytes 3076
  7.2 55.9 %all-gather.3.cloned.1.call-start = ((), (), s32[]{:S(2)}) async-start(), calls=%async_computation.2 | async-start | bytes 2621440 | tf_op jit(solution)/shard_map/all_gather | solution.py:73
  7.9 152.5 %all-gather.5.cloned.1.call-start = ((), (), s32[]{:S(2)}) async-start(), calls=%async_computation.3 | async-start | bytes 4259840 | tf_op jit(solution)/shard_map/all_gather | solution.py:86
  9.5 784.5 %reduce-scatter.5.cloned.1.call-start = ((), (), s32[]{:S(2)}) async-start(), calls=%async_computation.5 | async-start | bytes 8519680 | tf_op jit(solution)/shard_map/reduce_scatter | solution.py:111
  379.6 467.6 %reduce-scatter.3.cloned.1.call-start = ((), (), s32[]{:S(2)}) async-start(), calls=%async_computation.4 | async-start | bytes 2621440 | tf_op jit(solution)/shard_map/reduce_scatter | solution.py:110
Sparse Core Ops, SparseCore 0:
  9.8 53.2 all-gather.2
  67.4 93.0 all-gather.4
  379.7 414.1 reduce-scatter.4
  796.9 50.2 reduce-scatter.2
where the time goes:
time: 856 us; the launch traced here: 854 us
  waiting for transfers between devices  604 us (71%)
  other arithmetic  122 us (14%)
  matrix products  74.5 us (9%)
  local copies, waits for them, and re-layouts  38.2 us (4%)
  between operations  13.8 us (2%)
    reduce_scatter x1, waiting for transfers between devices, per_device(): panel_rcv = lax.psum_scatter(other, 'src', scatter_dimension=2, tiled=True)  410 us
    all_gather x1, waiting for transfers between devices, per_device(): shard_piece = lax.all_gather(rcv_spec, 'src', axis=2, tiled=True)  97.3 us
    reduce_scatter x1, waiting for transfers between devices, per_device(): lax.psum_scatter(src_total, 'rcv', scatter_dimension=2, tiled=True)  51.6 us
    all_gather x1, waiting for transfers between devices, per_device(): src_full = lax.all_gather(src_spec, 'rcv', axis=2, tiled=True)  44 us
    dot_general x16, matrix products, cross_block(): jnp.einsum('cgwfs,cgwfr->gfsr', swapped, rcv_five, preferred_element_type...  40 us
    dot_general x16, matrix products, cross_block(): jnp.einsum('cgwfs,cgwfr->gfsr', src_five, rcv_five, preferred_element_typ...  22.9 us
    another operation x16, other arithmetic, receiver_outer(): return jnp.transpose(jnp.stack([panel_re, panel_im]), (2, 0, 1, 3))  20.8 us
    convert_element_type x16, other arithmetic, source_slant(): sin_b = rcv_sin.astype(jnp.bfloat16)  20.1 us
  transfers between devices with their start and end apart: 4, of which 4 were waited for; matrix products, arithmetic and copies ran while one was open for 2% of the time, Pallas kernels for 0%

commit v1 on v0

v1 whole, which is shorter than its diff:
```python
import functools
import math

import jax
import jax.numpy as jnp
from jax import lax
from jax.experimental import pallas as pl
from jax.experimental.pallas import tpu as pltpu
from jax.sharding import PartitionSpec as P

MESH = pl.DeviceIdType.MESH
N_SRC = 64
N_RCV = 4
N_DEV = 256
N_FREQ = 256
N_SLOW = 16
N_S = 4096
N_R = 1024
SB = 64
RB = 256
TILE = 256
LAG_MID = 256


def lag_kernel(table_ref, pos_ref, src_ref, rcv_ref):
    n_pos = SB + RB
    n_hi = table_ref.shape[1] // 128
    pieces = [table_ref[:, h * 128:(h + 1) * 128] for h in range(n_hi)]
    table = jnp.concatenate(pieces, axis=0).astype(jnp.float32) - float(LAG_MID)
    pos = pos_ref[...]
    low = lax.rem(pos, 128)
    high = lax.div(pos, 128)
    pick = (lax.broadcasted_iota(jnp.int32, (128, n_pos), 0) == low).astype(jnp.float32)
    rows = jnp.dot(
        table.astype(jnp.bfloat16), pick.astype(jnp.bfloat16), preferred_element_type=jnp.float32
    )
    total = jnp.zeros((N_SLOW, n_pos), jnp.float32)
    for h in range(n_hi):
        total = total + jnp.where(high == h, rows[h * N_SLOW:(h + 1) * N_SLOW], 0.0)
    src = total[:, RB:RB + SB]
    src = jnp.concatenate([src[:8], src[8:]], axis=1)
    src_ref[...] = src.astype(jnp.bfloat16)
    rcv_ref[...] = total[:, :RB].astype(jnp.bfloat16)


def own_lags(lag_table, src_pos, rcv_pos):
    pos = jnp.concatenate([rcv_pos, src_pos])[None, :]
    return pl.pallas_call(
        lag_kernel,
        out_shape=(
            jax.ShapeDtypeStruct((8, 128), jnp.bfloat16),
            jax.ShapeDtypeStruct((N_SLOW, RB), jnp.bfloat16),
        ),
        name="own_lags",
    )(lag_table, pos)


def spread_kernel(s_ref, r_ref, so_ref, ro_ref, ssem, rsem, lsem, ssem2, rsem2, lsem2):
    i = lax.axis_index("src")
    j = lax.axis_index("rcv")
    own = lax.div(i, 16) == j
    away = jnp.logical_not(own)
    barrier = pltpu.get_barrier_semaphore()
    from_rcv = lax.div(i, 16)

    def greet(d, carry):
        peer = lax.rem(i + d, N_SRC)
        pl.semaphore_signal(barrier, inc=1, device_id=(peer, from_rcv), device_id_type=MESH)
        return carry

    lax.fori_loop(1, N_SRC, greet, 0)
    for d in range(1, N_RCV):
        pl.semaphore_signal(
            barrier, inc=1, device_id=(i, lax.rem(j + d, N_RCV)), device_id_type=MESH
        )

    @pl.when(away)
    def _():
        pl.semaphore_signal(barrier, inc=1, device_id=(i, from_rcv), device_id_type=MESH)
        pl.semaphore_wait(barrier, N_SRC + N_RCV - 1)

    @pl.when(own)
    def _():
        pl.semaphore_wait(barrier, N_SRC + N_RCV - 2)

    local = pltpu.make_async_copy(r_ref.at[j], ro_ref.at[j], lsem2)
    local.start()

    def send(d, carry):
        local_f = lax.rem(lax.rem(i, 16) * 4 + j + d, SB)
        dest_i = 16 * j + lax.div(local_f, 4)
        dest_j = lax.rem(local_f, 4)
        pltpu.make_async_remote_copy(
            s_ref.at[local_f], so_ref.at[i], ssem, rsem,
            device_id=(dest_i, dest_j), device_id_type=MESH,
        ).start()
        return carry

    for d in range(1, N_RCV):
        peer = lax.rem(j + d, N_RCV)
        pltpu.make_async_remote_copy(
            r_ref.at[peer], ro_ref.at[j], ssem2, rsem2, device_id=(i, peer), device_id_type=MESH
        ).start()
    lax.fori_loop(1, SB, send, 0)
    first = lax.rem(i, 16) * 4 + j
    whole = pltpu.make_async_remote_copy(
        s_ref, so_ref, ssem, rsem, device_id=(i, j), device_id_type=MESH
    )
    part = pltpu.make_async_remote_copy(
        s_ref.at[pl.ds(0, SB - 1)], so_ref.at[pl.ds(0, SB - 1)], ssem, rsem,
        device_id=(i, j), device_id_type=MESH,
    )

    @pl.when(own)
    def _():
        keep = pltpu.make_async_copy(s_ref.at[first], so_ref.at[i], lsem)
        keep.start()
        keep.wait()
        part.wait_send()
        part.wait_recv()

    @pl.when(away)
    def _():
        pltpu.make_async_remote_copy(
            s_ref.at[first], so_ref.at[i], ssem, rsem,
            device_id=(16 * j + lax.rem(i, 16), j), device_id_type=MESH,
        ).start()
        whole.wait_send()
        whole.wait_recv()

    local.wait()
    rest = pltpu.make_async_remote_copy(
        r_ref.at[pl.ds(0, N_RCV - 1)], ro_ref.at[pl.ds(0, N_RCV - 1)], ssem2, rsem2,
        device_id=(i, j), device_id_type=MESH,
    )
    rest.wait_send()
    rest.wait_recv()


def spread(src_pack, rcv_pack):
    return pl.pallas_call(
        spread_kernel,
        out_shape=(
            jax.ShapeDtypeStruct(src_pack.shape, src_pack.dtype),
            jax.ShapeDtypeStruct(rcv_pack.shape, rcv_pack.dtype),
        ),
        in_specs=[pl.BlockSpec(memory_space=pltpu.VMEM)] * 2,
        out_specs=(pl.BlockSpec(memory_space=pltpu.VMEM),) * 2,
        scratch_shapes=[pltpu.SemaphoreType.DMA] * 6,
        compiler_params=pltpu.CompilerParams(has_side_effects=True, collective_id=1),
        name="spread",
    )(src_pack, rcv_pack)


def unit_circle(m):
    quad = lax.shift_right_logical(m + 64, 7)
    x = (m - quad * 128).astype(jnp.float32) * (math.pi / N_FREQ)
    x2 = x * x
    sin = x * (1.0 + x2 * (-1 / 6 + x2 * (1 / 120 + x2 * (-1 / 5040 + x2 * (1 / 362880)))))
    cos = 1.0 + x2 * (-0.5 + x2 * (1 / 24 + x2 * (-1 / 720 + x2 * (1 / 40320))))
    odd = (quad & 1) == 1
    base_cos = jnp.where(odd, sin, cos)
    base_sin = jnp.where(odd, cos, sin)
    turn = quad & 3
    cos_out = jnp.where((turn == 1) | (turn == 2), -base_cos, base_cos)
    sin_out = jnp.where(turn >= 2, -base_sin, base_sin)
    return cos_out, sin_out


def phases(lag, freq):
    m = ((lag + float(LAG_MID)).astype(jnp.int32) * freq) & (2 * N_FREQ - 1)
    return unit_circle(m)


def cross_kernel(
    freq_ref, s_ref, r_ref, ms_ref, mr_ref,
    left_ref, er_ref, w_ref, es_ref, g_ref, acc_ref, turn_ref,
):
    freq = freq_ref[0]
    bf = jnp.bfloat16
    f32 = jnp.float32
    rcv = jnp.concatenate([r_ref[q, :32] for q in range(N_RCV)], axis=1).astype(f32)
    swapped = jnp.concatenate([-rcv[16:], rcv[:16]], axis=0)
    seg = (lax.broadcasted_iota(jnp.int32, rcv.shape, 0) & 15) < 8
    stack = jnp.concatenate(
        [
            jnp.where(seg, rcv, 0.0),
            jnp.where(seg, swapped, 0.0),
            jnp.where(seg, 0.0, rcv),
            jnp.where(seg, 0.0, swapped),
        ],
        axis=0,
    )
    turned = jnp.transpose(stack)
    block = lax.broadcasted_iota(jnp.int32, turned.shape, 1) // 32
    for v in range(4):
        left_ref[v] = jnp.where(block == v, turned, 0.0).astype(bf)
    lag_r = jnp.concatenate([r_ref[q, 32:48] for q in range(N_RCV)], axis=1).astype(f32)
    cos_r, sin_r = phases(lag_r, freq)
    er_ref[0] = jnp.concatenate([cos_r, sin_r], axis=0)
    er_ref[1] = jnp.concatenate([-sin_r, cos_r], axis=0)
    lane = lax.broadcasted_iota(jnp.int32, (24, 128), 1) < 64

    acc_ref[...] = jnp.zeros_like(acc_ref)

    def step(t, carry):
        parts = []
        for pair in range(2):
            a = s_ref[4 * t + 2 * pair].astype(f32)
            b = s_ref[4 * t + 2 * pair + 1].astype(f32)
            low = jnp.where(lane, a, pltpu.roll(b, 64, 1))
            high = jnp.where(lane, pltpu.roll(a, 64, 1), b)
            parts.append((low, high))
        low = jnp.concatenate([parts[0][0], parts[1][0]], axis=1)
        high = jnp.concatenate([parts[0][1], parts[1][1]], axis=1)
        weights = jnp.concatenate([low[:16], high[:16]], axis=0).astype(bf)
        weights = jnp.concatenate([weights] * 4, axis=0)
        lag_s = jnp.concatenate([low[16:], high[16:]], axis=0)
        cos_s, sin_s = phases(lag_s, freq)
        for q in range(4):
            rows = slice(q * 256, (q + 1) * 256)
            re0 = jnp.dot(left_ref[0, rows], weights, preferred_element_type=f32)
            im0 = jnp.dot(left_ref[1, rows], weights, preferred_element_type=f32)
            re1 = jnp.dot(left_ref[2, rows], weights, preferred_element_type=f32)
            im1 = jnp.dot(left_ref[3, rows], weights, preferred_element_type=f32)
            inv0 = lax.rsqrt(jnp.maximum(re0 * re0 + im0 * im0, 1.0))
            inv1 = lax.rsqrt(jnp.maximum(re1 * re1 + im1 * im1, 1.0))
            g_ref[0, rows] = (re0 * inv0 + re1 * inv1).astype(bf)
            g_ref[1, rows] = (im0 * inv0 + im1 * inv1).astype(bf)
        sums = jnp.dot(er_ref[0].astype(bf), g_ref[0], preferred_element_type=f32)
        sums = sums + jnp.dot(er_ref[1].astype(bf), g_ref[1], preferred_element_type=f32)
        cos_b = cos_s.astype(bf)
        sin_b = sin_s.astype(bf)
        es0 = jnp.concatenate([cos_b, -sin_b], axis=0)
        es1 = jnp.concatenate([sin_b, cos_b], axis=0)
        nt = (((1,), (1,)), ((), ()))
        acc_ref[...] += lax.dot_general(
            es0, g_ref[0], nt, preferred_element_type=f32
        ) + lax.dot_general(es1, g_ref[1], nt, preferred_element_type=f32)
        factor = 0.5 / math.sqrt(N_R)
        sum_re, sum_im = sums[:16], sums[16:]
        out_re = (sum_re * cos_s + sum_im * sin_s) * factor
        out_im = (sum_im * cos_s - sum_re * sin_s) * factor
        both = jnp.concatenate([out_re, out_im], axis=0)
        wide = jnp.concatenate([both] * 4, axis=0)
        turn_ref[...] = jnp.transpose(wide).reshape(16, 16, 128)
        part = lax.broadcasted_iota(jnp.int32, (16, 4, 128), 2) // 32
        msg = jnp.where(
            part < 2,
            jnp.where(part == 0, turn_ref[:, 0:4], turn_ref[:, 4:8]),
            jnp.where(part == 2, turn_ref[:, 8:12], turn_ref[:, 12:16]),
        )
        ms_ref[pl.ds(t * 16, 16)] = msg.astype(bf)
        return carry

    lax.fori_loop(0, N_S // TILE, step, 0)
    factor = 0.5 / math.sqrt(N_S)
    acc_re, acc_im = acc_ref[:16], acc_ref[16:]
    out_re = (acc_re * cos_r - acc_im * sin_r) * factor
    out_im = (acc_re * sin_r + acc_im * cos_r) * factor
    both = jnp.concatenate([out_re, out_im], axis=0).astype(bf)
    for q in range(N_RCV):
        mr_ref[q] = both[:, q * RB:(q + 1) * RB]


def cross(freq, src_all, rcv_all):
    return pl.pallas_call(
        cross_kernel,
        out_shape=(
            jax.ShapeDtypeStruct((N_DEV, 4, 128), jnp.bfloat16),
            jax.ShapeDtypeStruct((N_RCV, 2 * N_SLOW, RB), jnp.bfloat16),
        ),
        in_specs=[
            pl.BlockSpec(memory_space=pltpu.SMEM),
            pl.BlockSpec(memory_space=pltpu.VMEM),
            pl.BlockSpec(memory_space=pltpu.VMEM),
        ],
        out_specs=(pl.BlockSpec(memory_space=pltpu.VMEM),) * 2,
        scratch_shapes=[
            pltpu.VMEM((4, N_R, 128), jnp.bfloat16),
            pltpu.VMEM((2, 2 * N_SLOW, N_R), jnp.float32),
            pltpu.VMEM((128, TILE), jnp.bfloat16),
            pltpu.VMEM((2, 2 * N_SLOW, TILE), jnp.float32),
            pltpu.VMEM((2, N_R, TILE), jnp.bfloat16),
            pltpu.VMEM((2 * N_SLOW, N_R), jnp.float32),
            pltpu.VMEM((16, 16, 128), jnp.float32),
        ],
        name="cross",
    )(freq, src_all, rcv_all)


def collect_kernel(s_ref, r_ref, so_ref, ro_ref, ssem, rsem, lsem, ssem2, rsem2, lsem2):
    i = lax.axis_index("src")
    j = lax.axis_index("rcv")
    me = i * N_RCV + j
    keep = pltpu.make_async_copy(s_ref.at[me], so_ref.at[me], lsem)
    keep2 = pltpu.make_async_copy(r_ref.at[j], ro_ref.at[j], lsem2)
    keep.start()
    keep2.start()
    barrier = pltpu.get_barrier_semaphore()

    def greet(d, carry):
        peer = lax.rem(me + d, N_DEV)
        pl.semaphore_signal(
            barrier, inc=1, device_id=(lax.div(peer, N_RCV), lax.rem(peer, N_RCV)),
            device_id_type=MESH,
        )
        return carry

    lax.fori_loop(1, N_DEV, greet, 0)
    pl.semaphore_wait(barrier, N_DEV - 1)
    for d in range(1, N_RCV):
        peer = lax.rem(j + d, N_RCV)
        pltpu.make_async_remote_copy(
            r_ref.at[peer], ro_ref.at[j], ssem2, rsem2, device_id=(i, peer), device_id_type=MESH
        ).start()

    def send(d, carry):
        peer = lax.rem(me + d, N_DEV)
        pltpu.make_async_remote_copy(
            s_ref.at[peer], so_ref.at[me], ssem, rsem,
            device_id=(lax.div(peer, N_RCV), lax.rem(peer, N_RCV)), device_id_type=MESH,
        ).start()
        return carry

    lax.fori_loop(1, N_DEV, send, 0)
    keep.wait()
    keep2.wait()
    rest2 = pltpu.make_async_remote_copy(
        r_ref.at[pl.ds(0, N_RCV - 1)], ro_ref.at[pl.ds(0, N_RCV - 1)], ssem2, rsem2,
        device_id=(i, j), device_id_type=MESH,
    )
    rest = pltpu.make_async_remote_copy(
        s_ref.at[pl.ds(0, N_DEV - 1)], so_ref.at[pl.ds(0, N_DEV - 1)], ssem, rsem,
        device_id=(i, j), device_id_type=MESH,
    )
    rest2.wait_send()
    rest2.wait_recv()
    rest.wait_send()
    rest.wait_recv()


def collect(src_msg, rcv_msg):
    return pl.pallas_call(
        collect_kernel,
        out_shape=(
            jax.ShapeDtypeStruct(src_msg.shape, src_msg.dtype),
            jax.ShapeDtypeStruct(rcv_msg.shape, rcv_msg.dtype),
        ),
        in_specs=[pl.BlockSpec(memory_space=pltpu.VMEM)] * 2,
        out_specs=(pl.BlockSpec(memory_space=pltpu.VMEM),) * 2,
        scratch_shapes=[pltpu.SemaphoreType.DMA] * 6,
        compiler_params=pltpu.CompilerParams(has_side_effects=True, collective_id=2),
        name="collect",
    )(src_msg, rcv_msg)


def arrange_kernel(m_ref, o_ref):
    q = lax.broadcasted_iota(jnp.int32, (512, 128), 0)
    k = lax.broadcasted_iota(jnp.int32, (512, 128), 1)
    p, c, s = q // 32, (q // 16) & 1, q & 15
    lane = (s // 4) * 32 + c * 16 + p
    total = jnp.zeros((512, N_FREQ), jnp.float32)
    nt = (((1,), (1,)), ((), ()))
    for row in range(4):
        pick = jnp.where((k == lane) & ((s & 3) == row), 1.0, 0.0).astype(jnp.bfloat16)
        total = total + lax.dot_general(
            pick, m_ref[:, row, :], nt, preferred_element_type=jnp.float32
        )
    o_ref[...] = total


def arrange(msg):
    return pl.pallas_call(
        arrange_kernel,
        out_shape=jax.ShapeDtypeStruct((512, N_FREQ), jnp.float32),
        name="arrange",
    )(msg)


def per_device(src_spec, rcv_spec, lag_table, src_pos, rcv_pos):
    lag_s, lag_r = own_lags(lag_table, src_pos, rcv_pos)
    src_rows = jnp.transpose(src_spec, (2, 1, 0, 3)).reshape(SB, 16, 128)
    src_pack = jnp.concatenate([src_rows, jnp.broadcast_to(lag_s, (SB, 8, 128))], axis=1)
    rcv_rows = jnp.transpose(rcv_spec, (2, 0, 1, 3)).reshape(N_RCV, 32, RB)
    rcv_pack = jnp.concatenate([rcv_rows, jnp.broadcast_to(lag_r, (N_RCV, 16, RB))], axis=1)
    src_all, rcv_all = spread(src_pack, rcv_pack)
    freq = (lax.axis_index("src") * N_RCV + lax.axis_index("rcv")).astype(jnp.int32).reshape(1)
    src_msg, rcv_msg = cross(freq, src_all, rcv_all)
    src_got, rcv_got = collect(src_msg, rcv_msg)
    panel_src = arrange(src_got).reshape(N_SLOW, 2, 16, N_FREQ)
    rcv_got = rcv_got.reshape(N_RCV, 2, N_SLOW, RB)
    panel_rcv = jnp.transpose(rcv_got, (2, 1, 0, 3)).astype(jnp.float32)
    return (panel_src, panel_rcv)


def solution(mesh):
    placed = (P(None, None, "rcv", "src"), P(None, None, "src", "rcv"), P(), P("src"), P("rcv"))
    return jax.shard_map(
        per_device,
        mesh=mesh,
        in_specs=placed,
        out_specs=(P(None, None, ("src", "rcv"), None), P(None, None, "src", "rcv")),
        check_vma=False,
    )
```

time: 856 us -> 87.4 us (0.10)
  waiting for transfers between devices: 604 us -> 0 us
  other arithmetic: 122 us -> 2.19 us
  Pallas kernels: 0 us -> 81.4 us
  matrix products: 74.5 us -> 0 us
  local copies, waits for them, and re-layouts: 38.2 us -> 2.86 us
  between operations: 13.8 us -> 0.72 us
    reduce_scatter x2 -> x0, waiting for transfers between devices: 462 us -> none  [the longest x1 410 us: per_device(): panel_rcv = lax.psum_scatter(other, 'src', scatter_dimension=2, tiled=True)]
    all_gather x2 -> x0, waiting for transfers between devices: 141 us -> none  [the longest x1 97.3 us: per_device(): shard_piece = lax.all_gather(rcv_spec, 'src', axis=2, tiled=True)]
    pallas_call x0 -> x5, Pallas kernels: none -> 81.4 us  [the longest x1 30.1 us: collect(): pl.pallas_call(collect_kernel, out_shape=(jax.ShapeDtypeStruct(src_msg.sh...]
    dot_general x64 -> x0, matrix products: 74.5 us -> none  [the longest x16 40 us: cross_block(): jnp.einsum('cgwfs,cgwfr->gfsr', swapped, rcv_five, preferred_element_type...]
    convert_element_type x48 -> x0, other arithmetic: 34.9 us -> none  [the longest x16 20.1 us: source_slant(): sin_b = rcv_sin.astype(jnp.bfloat16)]
    neg x32 -> x0, other arithmetic: 26.1 us -> none  [the longest x16 17 us: source_slant(): bottom = jnp.concatenate([-sin_b, cos_b], axis=2)]
    dynamic_update_slice x32 -> x0, other arithmetic: 25.1 us -> none  [the longest x16 13.4 us: inner(): other = lax.dynamic_update_slice_in_dim(totals[1], rcv_part, offset, 2)]
    another operation x16 -> x0, other arithmetic: 20.8 us -> none  [receiver_outer(): return jnp.transpose(jnp.stack([panel_re, panel_im]), (2, 0, 1, 3))]
  transfers between devices with their start and end apart: 4 -> 0, of which waited for: 4 -> 0; matrix products, arithmetic and copies ran while one was open for 2% -> 0% of each run, Pallas kernels for 0% -> 0%
where the time goes in v1:
time: 87.4 us; the launch traced here: 87.1 us
  Pallas kernels  81.4 us (93%)
  local copies, waits for them, and re-layouts  2.86 us (3%)
  other arithmetic  2.19 us (3%)
    pallas_call x1, Pallas kernels, collect(): pl.pallas_call(collect_kernel, out_shape=(jax.ShapeDtypeStruct(src_msg.sh...  30.1 us
    pallas_call x1, Pallas kernels, cross(): pl.pallas_call(cross_kernel, out_shape=(jax.ShapeDtypeStruct((N_DEV, 4, 1...  24.7 us
    pallas_call x1, Pallas kernels, spread(): pl.pallas_call(spread_kernel, out_shape=(jax.ShapeDtypeStruct(src_pack.sh...  21.8 us
    pallas_call x1, Pallas kernels, arrange(): pl.pallas_call(arrange_kernel, out_shape=jax.ShapeDtypeStruct((512, N_FRE...  2.81 us
    pallas_call x1, Pallas kernels, own_lags(): pl.pallas_call(lag_kernel, out_shape=(jax.ShapeDtypeStruct((8, 128), jnp....  2.05 us

profile of v1, /device:TPU:1, one launch (start us, length us, event | category | flops | bytes accessed | tf_op | source)
XLA Modules:
  0.0 87.1 jit_solution(10904926821118305776)
XLA Ops:
  0.6 0.0 copy-start
  0.6 0.8 pad_add_fusion
  1.4 0.6 broadcast_in_dim.9.pos_ref
  2.0 2.0 %own_lags.1 = (bf16[8,128]{1,0:T(8,128)(2,1)}, bf16[16,256]{1,0:T(8,128)(2,1)}) custom-call(s32[16,8192]{1,0:T(8,128)} %table_ref.1, s32[1,320]{1,0:T(1,128)} %broadcast_in_dim.9.pos_ref), custom_call_target="tpu_custom_call" | custom-call | tf_op jit(solution)/shard_map/own_lags/pallas_call | solution.py:48
  4.0 0.7 broadcast_in_dim.10
  4.7 0.0 copy-done
  4.8 0.5 copy.7
  5.3 0.2 reshape.20
  5.6 0.0 copy-start.3
  5.6 0.0 copy-start.2
  5.6 0.8 pad_maximum_fusion.s_ref
  6.4 0.0 copy-done.3
  6.4 0.0 copy-done.2
  6.4 0.6 pad_maximum_fusion.1.r_ref
  7.1 21.8 %spread.1 = (bf16[64,24,128]{2,1,0:T(8,128)(2,1)}, bf16[4,48,256]{2,1,0:T(8,128)(2,1)}) custom-call(bf16[64,24,128]{2,1,0:T(8,128)(2,1)} %pad_maximum_fusion.s_ref, bf16[4,48,256]{2,1,0:T(8,128)(2,1)} %pad_maximum_fusion.1.r_ref), custom_call_target="tpu_custom_call" | custom-call | tf_op jit(solution)/shard_map/spread/pallas_call | solution.py:141
  28.8 24.7 %cross.1 = (bf16[256,4,128]{2,1,0:T(4,128)(2,1)}, bf16[4,32,256]{2,1,0:T(8,128)(2,1)}) custom-call(s32[1]{0:T(128)} %bitcast.freq_ref, bf16[64,24,128]{2,1,0:T(8,128)(2,1)} %get-tuple-element.12.s_ref, bf16[4,48,256]{2,1,0:T(8,128)(2,1)} %get-tuple-element.13.r_ref), custom_call_target="tpu_custom_call" | custom-call | tf_op jit(solution)/shard_map/cross/pallas_call | solution.py:267
  53.5 30.1 %collect.1 = (bf16[256,4,128]{2,1,0:T(4,128)(2,1)}, bf16[4,32,256]{2,1,0:T(8,128)(2,1)}) custom-call(bf16[256,4,128]{2,1,0:T(4,128)(2,1)} %get-tuple-element.14.s_ref, bf16[4,32,256]{2,1,0:T(8,128)(2,1)} %get-tuple-element.15.r_ref), custom_call_target="tpu_custom_call" | custom-call | tf_op jit(solution)/shard_map/collect/pallas_call | solution.py:344
  83.6 0.0 copy-start.1
  83.6 2.8 %arrange.1 = f32[512,256]{1,0:T(8,128)} custom-call(bf16[256,4,128]{2,1,0:T(4,128)(2,1)} %get-tuple-element.16.m_ref), custom_call_target="tpu_custom_call" | custom-call | tf_op jit(solution)/shard_map/arrange/pallas_call | solution.py:374
  86.4 0.0 copy-done.1
  86.4 0.7 copy.11
  (2 shorter events, 0.0 us)
Async XLA Ops:
  0.6 4.1 %copy-start = (bf16[2,16,64,64]{3,2,1,0:T(8,128)(2,1)S(1)}, bf16[2,16,64,64]{3,2,1,0:T(8,128)(2,1)}, u32[]{:S(2)}) copy-start(bf16[2,16,64,64]{3,2,1,0:T(8,128)(2,1)} %param.5) | copy-start | bytes 786436
  5.6 0.8 copy-start.3
  5.6 0.8 copy-start.2
  83.6 2.8 %copy-start.1 = (bf16[4,32,256]{2,1,0:T(8,128)(2,1)S(1)}, bf16[4,32,256]{2,1,0:T(8,128)(2,1)}, u32[]{:S(2)}) copy-start(bf16[4,32,256]{2,1,0:T(8,128)(2,1)} %get-tuple-element.17) | copy-start | bytes 196612

commit v2 on v0

v2 whole, which is shorter than its diff:
```python
import functools
import math

import jax
import jax.numpy as jnp
from jax import lax
from jax.experimental import pallas as pl
from jax.experimental.pallas import tpu as pltpu
from jax.sharding import PartitionSpec as P

MESH = pl.DeviceIdType.MESH
N_SRC = 64
N_RCV = 4
N_DEV = 256
N_FREQ = 256
N_SLOW = 16
N_S = 4096
N_R = 1024
SB = 64
RB = 256
TILE = 256
LAG_MID = 256


def own_lags(table_ref, pos_ref):
    n_pos = SB + RB
    n_hi = table_ref.shape[1] // 128
    pieces = [table_ref[:, h * 128:(h + 1) * 128] for h in range(n_hi)]
    table = jnp.concatenate(pieces, axis=0).astype(jnp.float32) - float(LAG_MID)
    pos = pos_ref[...]
    low = pos & 127
    high = lax.shift_right_logical(pos, 7)
    pick = (lax.broadcasted_iota(jnp.int32, (128, n_pos), 0) == low).astype(jnp.float32)
    rows = jnp.dot(
        table.astype(jnp.bfloat16), pick.astype(jnp.bfloat16), preferred_element_type=jnp.float32
    )
    total = jnp.zeros((N_SLOW, n_pos), jnp.float32)
    for h in range(n_hi):
        total = total + jnp.where(high == h, rows[h * N_SLOW:(h + 1) * N_SLOW], 0.0)
    src = total[:, RB:RB + SB]
    src = jnp.concatenate([src[:8], src[8:]], axis=1)
    return src.astype(jnp.bfloat16), total[:, :RB].astype(jnp.bfloat16)


def unit_circle(m):
    quad = lax.shift_right_logical(m + 64, 7)
    x = (m - quad * 128).astype(jnp.float32) * (math.pi / N_FREQ)
    x2 = x * x
    sin = x * (1.0 + x2 * (-1 / 6 + x2 * (1 / 120 + x2 * (-1 / 5040 + x2 * (1 / 362880)))))
    cos = 1.0 + x2 * (-0.5 + x2 * (1 / 24 + x2 * (-1 / 720 + x2 * (1 / 40320))))
    odd = (quad & 1) == 1
    base_cos = jnp.where(odd, sin, cos)
    base_sin = jnp.where(odd, cos, sin)
    turn = quad & 3
    cos_out = jnp.where((turn == 1) | (turn == 2), -base_cos, base_cos)
    sin_out = jnp.where(turn >= 2, -base_sin, base_sin)
    return cos_out, sin_out


def phases(lag, freq):
    m = ((lag + float(LAG_MID)).astype(jnp.int32) * freq) & (2 * N_FREQ - 1)
    return unit_circle(m)


def prepare_receivers(r_ref, left_ref, er_ref, freq):
    bf = jnp.bfloat16
    f32 = jnp.float32
    rcv = jnp.concatenate([r_ref[q, :32] for q in range(N_RCV)], axis=1).astype(f32)
    swapped = jnp.concatenate([-rcv[16:], rcv[:16]], axis=0)
    seg = (lax.broadcasted_iota(jnp.int32, rcv.shape, 0) & 15) < 8
    variants = [
        jnp.where(seg, rcv, 0.0),
        jnp.where(seg, swapped, 0.0),
        jnp.where(seg, 0.0, rcv),
        jnp.where(seg, 0.0, swapped),
    ]
    turned = jnp.transpose(jnp.concatenate(variants, axis=0))
    for v in range(4):
        left_ref[:, v] = turned[:, 32 * v:32 * v + 32].reshape(N_R // 16, 16, 32).astype(bf)
    lag_r = jnp.concatenate([r_ref[q, 32:48] for q in range(N_RCV)], axis=1).astype(f32)
    cos_r, sin_r = phases(lag_r, freq)
    upper = jnp.concatenate([cos_r, sin_r], axis=0).astype(bf)
    lower = jnp.concatenate([-sin_r, cos_r], axis=0).astype(bf)
    for q in range(4):
        cols = slice(q * RB, (q + 1) * RB)
        er_ref[q] = jnp.concatenate([upper[:, cols], lower[:, cols]], axis=1)
    return cos_r, sin_r


def prepare_sources(s_ref, w_ref, ph_ref, freq):
    f32 = jnp.float32
    lane = lax.broadcasted_iota(jnp.int32, (24, 128), 1) < 64

    def prep(t, carry):
        parts = []
        for pair in range(2):
            a = s_ref[4 * t + 2 * pair].astype(f32)
            b = s_ref[4 * t + 2 * pair + 1].astype(f32)
            low = jnp.where(lane, a, pltpu.roll(b, 64, 1))
            high = jnp.where(lane, pltpu.roll(a, 64, 1), b)
            parts.append((low, high))
        low = jnp.concatenate([parts[0][0], parts[1][0]], axis=1)
        high = jnp.concatenate([parts[0][1], parts[1][1]], axis=1)
        w_ref[t] = jnp.concatenate([low[:16], high[:16]], axis=0).astype(jnp.bfloat16)
        lag_s = jnp.concatenate([low[16:], high[16:]], axis=0)
        cos_s, sin_s = phases(lag_s, freq)
        ph_ref[t] = jnp.concatenate([cos_s, sin_s], axis=0)
        return carry

    lax.fori_loop(0, N_S // TILE, prep, 0)


def cross_chunk(left_ref, weights, g_ref, q):
    f32 = jnp.float32
    bf = jnp.bfloat16
    halves = []
    for h in range(2):
        lhs = left_ref[q * 16 + 8 * h:q * 16 + 8 * h + 8].reshape(512, 32)
        halves.append(jnp.dot(lhs, weights, preferred_element_type=f32))
    for k in range(16):
        h, base = k % 2, (k // 2) * 64
        re0, im0, re1, im1 = [halves[h][base + v * 16:base + v * 16 + 16] for v in range(4)]
        inv0 = lax.rsqrt(jnp.maximum(re0 * re0 + im0 * im0, 1.0))
        inv1 = lax.rsqrt(jnp.maximum(re1 * re1 + im1 * im1, 1.0))
        row = 128 * h + 16 * (k // 2)
        g_ref[row:row + 16] = (re0 * inv0 + re1 * inv1).astype(bf)
        g_ref[RB + row:RB + row + 16] = (im0 * inv0 + im1 * inv1).astype(bf)


def slant_chunk(er_ref, es0, es1, g_ref, acc_ref, q):
    f32 = jnp.float32
    nt = (((1,), (1,)), ((), ()))
    cols = slice(q * RB, (q + 1) * RB)
    acc_ref[:, cols] += lax.dot_general(
        es0, g_ref[:RB], nt, preferred_element_type=f32
    ) + lax.dot_general(es1, g_ref[RB:], nt, preferred_element_type=f32)
    return jnp.dot(er_ref[q], g_ref[...], preferred_element_type=f32)


def message(sums, phase, turn_ref):
    factor = 0.5 / math.sqrt(N_R)
    cos_s, sin_s = phase[:16], phase[16:]
    sum_re, sum_im = sums[:16], sums[16:]
    out_re = (sum_re * cos_s + sum_im * sin_s) * factor
    out_im = (sum_im * cos_s - sum_re * sin_s) * factor
    both = jnp.concatenate([out_re, out_im], axis=0)
    wide = jnp.concatenate([both] * 4, axis=0)
    turn_ref[...] = jnp.transpose(wide).reshape(16, 16, 128)
    part = lax.broadcasted_iota(jnp.int32, (16, 4, 128), 2) // 32
    msg = jnp.where(
        part < 2,
        jnp.where(part == 0, turn_ref[:, 0:4], turn_ref[:, 4:8]),
        jnp.where(part == 2, turn_ref[:, 8:12], turn_ref[:, 12:16]),
    )
    return msg.astype(jnp.bfloat16)


def remote(src, dst, send_sem, recv_sem, dest):
    return pltpu.make_async_remote_copy(
        src, dst, send_sem, recv_sem, device_id=dest, device_id_type=MESH
    )


def panels_kernel(
    s_ref, r_ref, table_ref, pos_ref, so_ref, ro_ref,
    sp_ref, rp_ref, sa_ref, ra_ref, ms_ref, mr_ref,
    left_ref, er_ref, w_ref, ph_ref, g0_ref, g1_ref, g2_ref, g3_ref, sums_ref, acc_ref, turn_ref,
    in_send, in_recv, in_keep, rin_send, rin_recv, rin_keep,
    out_send, out_recv, out_keep, rout_send, rout_recv, rout_keep, ready,
):
    bf = jnp.bfloat16
    f32 = jnp.float32
    i = lax.axis_index("src")
    j = lax.axis_index("rcv")
    me = i * N_RCV + j
    freq = me
    g_refs = (g0_ref, g1_ref, g2_ref, g3_ref)
    n_tiles = N_S // TILE
    barrier = pltpu.get_barrier_semaphore()
    block = lax.div(i, 16)
    own = block == j
    away = jnp.logical_not(own)

    def greet(d, carry):
        pl.semaphore_signal(
            barrier, inc=1, device_id=(lax.rem(i + d, N_SRC), block), device_id_type=MESH
        )
        return carry

    lax.fori_loop(1, N_SRC, greet, 0)
    for d in range(1, N_RCV):
        pl.semaphore_signal(
            barrier, inc=1, device_id=(i, lax.rem(j + d, N_RCV)), device_id_type=MESH
        )

    @pl.when(away)
    def _():
        pl.semaphore_signal(barrier, inc=1, device_id=(i, block), device_id_type=MESH)

    lag_s, lag_r = own_lags(table_ref, pos_ref)
    sp_ref[:, :16] = s_ref[...]
    sp_ref[:, 16:] = jnp.broadcast_to(lag_s[None], (SB, 8, 128))
    rp_ref[:, :32] = r_ref[...]
    rp_ref[:, 32:] = jnp.broadcast_to(lag_r[None], (N_RCV, N_SLOW, RB))

    @pl.when(away)
    def _():
        pl.semaphore_wait(barrier, N_SRC + N_RCV - 1)

    @pl.when(own)
    def _():
        pl.semaphore_wait(barrier, N_SRC + N_RCV - 2)

    for d in range(1, N_RCV):
        pl.semaphore_signal(
            ready, inc=1, device_id=(i, lax.rem(j + d, N_RCV)), device_id_type=MESH
        )

    rin_local = pltpu.make_async_copy(rp_ref.at[j], ra_ref.at[j], rin_keep)
    rin_local.start()
    for d in range(1, N_RCV):
        peer = lax.rem(j + d, N_RCV)
        remote(rp_ref.at[peer], ra_ref.at[j], rin_send, rin_recv, (i, peer)).start()

    def send_in(d, carry):
        local_f = lax.rem(lax.rem(i, 16) * 4 + j + d, SB)
        dest = (16 * j + lax.div(local_f, 4), lax.rem(local_f, 4))
        remote(sp_ref.at[local_f], sa_ref.at[i], in_send, in_recv, dest).start()
        return carry

    lax.fori_loop(1, SB, send_in, 0)
    first_f = lax.rem(i, 16) * 4 + j

    @pl.when(own)
    def _():
        pltpu.make_async_copy(sp_ref.at[first_f], sa_ref.at[i], in_keep).start()

    @pl.when(away)
    def _():
        remote(
            sp_ref.at[first_f], sa_ref.at[i], in_send, in_recv, (16 * j + lax.rem(i, 16), j)
        ).start()

    acc_ref[...] = jnp.zeros_like(acc_ref)
    sums_ref[...] = jnp.zeros_like(sums_ref)
    g3_ref[...] = jnp.zeros_like(g3_ref)
    rin_local.wait()
    rin_rest = remote(
        rp_ref.at[pl.ds(0, N_RCV - 1)], ra_ref.at[pl.ds(0, N_RCV - 1)], rin_send, rin_recv, (i, j)
    )
    rin_rest.wait_send()
    rin_rest.wait_recv()
    cos_r, sin_r = prepare_receivers(ra_ref, left_ref, er_ref, freq)

    @pl.when(own)
    def _():
        pltpu.make_async_copy(sp_ref.at[first_f], sa_ref.at[i], in_keep).wait()
        part = remote(
            sp_ref.at[pl.ds(0, SB - 1)], sa_ref.at[pl.ds(0, SB - 1)], in_send, in_recv, (i, j)
        )
        part.wait_send()
        part.wait_recv()

    @pl.when(away)
    def _():
        whole = remote(sp_ref, sa_ref, in_send, in_recv, (i, j))
        whole.wait_send()
        whole.wait_recv()

    prepare_sources(sa_ref, w_ref, ph_ref, freq)
    pl.semaphore_wait(ready, N_RCV - 1)

    first = lax.div(me, 16) + 1

    def tile(n):
        return lax.rem(first + n + n_tiles, n_tiles)

    def write(n, sums):
        t = tile(n)
        ms_ref[pl.ds(t * 16, 16)] = message(sums, ph_ref[t], turn_ref)

    def send_out(n, start):
        for d in range(start, 16):
            row = tile(n) * 16 + lax.rem(me + d, 16)
            dest = (lax.div(row, N_RCV), lax.rem(row, N_RCV))
            remote(ms_ref.at[row], so_ref.at[me], out_send, out_recv, dest).start()

    def slants(n):
        phase = ph_ref[tile(n)]
        cos_b = phase[:16].astype(bf)
        sin_b = phase[16:].astype(bf)
        es0 = jnp.concatenate([cos_b, -sin_b], axis=0)
        es1 = jnp.concatenate([sin_b, cos_b], axis=0)
        return es0, es1

    def step(n, carry):
        @pl.when(n >= 2)
        def _():
            send_out(n - 2, 0)

        weights = w_ref[tile(n)]
        old = slants(n - 1)
        new = slants(n)
        cross_chunk(left_ref, weights, g0_ref, 0)
        sums = sums_ref[...] + slant_chunk(er_ref, *old, g3_ref, acc_ref, 3)
        write(n - 1, sums)
        cross_chunk(left_ref, weights, g1_ref, 1)
        sums = slant_chunk(er_ref, *new, g0_ref, acc_ref, 0)
        cross_chunk(left_ref, weights, g2_ref, 2)
        sums = sums + slant_chunk(er_ref, *new, g1_ref, acc_ref, 1)
        cross_chunk(left_ref, weights, g3_ref, 3)
        sums_ref[...] = sums + slant_chunk(er_ref, *new, g2_ref, acc_ref, 2)
        return carry

    lax.fori_loop(0, n_tiles, step, 0)
    last = slants(n_tiles - 1)
    sums = sums_ref[...] + slant_chunk(er_ref, *last, g3_ref, acc_ref, 3)
    write(n_tiles - 1, sums)
    send_out(n_tiles - 2, 0)
    factor = 0.5 / math.sqrt(N_S)
    acc_re, acc_im = acc_ref[:16], acc_ref[16:]
    out_re = (acc_re * cos_r - acc_im * sin_r) * factor
    out_im = (acc_re * sin_r + acc_im * cos_r) * factor
    both = jnp.concatenate([out_re, out_im], axis=0).astype(bf)
    for q in range(N_RCV):
        mr_ref[q] = both[:, q * RB:(q + 1) * RB]
    out_local = pltpu.make_async_copy(ms_ref.at[me], so_ref.at[me], out_keep)
    out_local.start()
    send_out(n_tiles - 1, 1)
    rout_local = pltpu.make_async_copy(mr_ref.at[j], ro_ref.at[j], rout_keep)
    rout_local.start()
    for d in range(1, N_RCV):
        peer = lax.rem(j + d, N_RCV)
        remote(mr_ref.at[peer], ro_ref.at[j], rout_send, rout_recv, (i, peer)).start()
    out_local.wait()
    rout_local.wait()
    rout_rest = remote(
        mr_ref.at[pl.ds(0, N_RCV - 1)], ro_ref.at[pl.ds(0, N_RCV - 1)], rout_send, rout_recv, (i, j)
    )
    rout_rest.wait_send()
    rout_rest.wait_recv()
    out_rest = remote(
        ms_ref.at[pl.ds(0, N_DEV - 1)], so_ref.at[pl.ds(0, N_DEV - 1)], out_send, out_recv, (i, j)
    )
    out_rest.wait_send()
    out_rest.wait_recv()


def panels(src_rows, rcv_rows, lag_table, pos):
    bf = jnp.bfloat16
    f32 = jnp.float32
    msg_s = (N_DEV, 4, 128)
    msg_r = (N_RCV, 2 * N_SLOW, RB)
    vmem = pl.BlockSpec(memory_space=pltpu.VMEM)
    return pl.pallas_call(
        panels_kernel,
        out_shape=(jax.ShapeDtypeStruct(msg_s, bf), jax.ShapeDtypeStruct(msg_r, bf)),
        in_specs=[vmem] * 4,
        out_specs=(vmem,) * 2,
        scratch_shapes=[
            pltpu.VMEM((SB, 24, 128), bf),
            pltpu.VMEM((N_RCV, 48, RB), bf),
            pltpu.VMEM((SB, 24, 128), bf),
            pltpu.VMEM((N_RCV, 48, RB), bf),
            pltpu.VMEM(msg_s, bf),
            pltpu.VMEM(msg_r, bf),
            pltpu.VMEM((N_R // 16, 4, 16, 32), bf),
            pltpu.VMEM((4, 2 * N_SLOW, 2 * RB), bf),
            pltpu.VMEM((N_S // TILE, 32, TILE), bf),
            pltpu.VMEM((N_S // TILE, 2 * N_SLOW, TILE), f32),
            pltpu.VMEM((2 * RB, TILE), bf),
            pltpu.VMEM((2 * RB, TILE), bf),
            pltpu.VMEM((2 * RB, TILE), bf),
            pltpu.VMEM((2 * RB, TILE), bf),
            pltpu.VMEM((2 * N_SLOW, TILE), f32),
            pltpu.VMEM((2 * N_SLOW, N_R), f32),
            pltpu.VMEM((16, 16, 128), f32),
        ] + [pltpu.SemaphoreType.DMA] * 12 + [pltpu.SemaphoreType.REGULAR],
        compiler_params=pltpu.CompilerParams(has_side_effects=True, collective_id=1),
        name="panels",
    )(src_rows, rcv_rows, lag_table, pos)


def arrange_kernel(m_ref, o_ref):
    q = lax.broadcasted_iota(jnp.int32, (512, 128), 0)
    k = lax.broadcasted_iota(jnp.int32, (512, 128), 1)
    p, c, s = q // 32, (q // 16) & 1, q & 15
    lane = (s // 4) * 32 + c * 16 + p
    total = jnp.zeros((512, N_FREQ), jnp.float32)
    nt = (((1,), (1,)), ((), ()))
    for row in range(4):
        pick = jnp.where((k == lane) & ((s & 3) == row), 1.0, 0.0).astype(jnp.bfloat16)
        total = total + lax.dot_general(
            pick, m_ref[:, row, :], nt, preferred_element_type=jnp.float32
        )
    o_ref[...] = total


def arrange(msg):
    return pl.pallas_call(
        arrange_kernel,
        out_shape=jax.ShapeDtypeStruct((512, N_FREQ), jnp.float32),
        name="arrange",
    )(msg)


def per_device(src_spec, rcv_spec, lag_table, src_pos, rcv_pos):
    pos = jnp.concatenate([rcv_pos, src_pos])[None, :]
    src_rows = jnp.transpose(src_spec, (2, 1, 0, 3)).reshape(SB, 16, 128)
    rcv_rows = jnp.transpose(rcv_spec, (2, 0, 1, 3)).reshape(N_RCV, 32, RB)
    src_got, rcv_got = panels(src_rows, rcv_rows, lag_table, pos)
    panel_src = arrange(src_got).reshape(N_SLOW, 2, 16, N_FREQ)
    rcv_got = rcv_got.reshape(N_RCV, 2, N_SLOW, RB)
    panel_rcv = jnp.transpose(rcv_got, (2, 1, 0, 3)).astype(jnp.float32)
    return (panel_src, panel_rcv)


def solution(mesh):
    placed = (P(None, None, "rcv", "src"), P(None, None, "src", "rcv"), P(), P("src"), P("rcv"))
    return jax.shard_map(
        per_device,
        mesh=mesh,
        in_specs=placed,
        out_specs=(P(None, None, ("src", "rcv"), None), P(None, None, "src", "rcv")),
        check_vma=False,
    )
```

time: 856 us -> 62.2 us (0.07)
  waiting for transfers between devices: 604 us -> 0 us
  other arithmetic: 122 us -> 0.01 us
  matrix products: 74.5 us -> 0 us
  Pallas kernels: 0 us -> 56.2 us
  local copies, waits for them, and re-layouts: 38.2 us -> 5.14 us
  between operations: 13.8 us -> 0.66 us
    reduce_scatter x2 -> x0, waiting for transfers between devices: 462 us -> none  [the longest x1 410 us: per_device(): panel_rcv = lax.psum_scatter(other, 'src', scatter_dimension=2, tiled=True)]
    all_gather x2 -> x0, waiting for transfers between devices: 141 us -> none  [the longest x1 97.3 us: per_device(): shard_piece = lax.all_gather(rcv_spec, 'src', axis=2, tiled=True)]
    dot_general x64 -> x0, matrix products: 74.5 us -> none  [the longest x16 40 us: cross_block(): jnp.einsum('cgwfs,cgwfr->gfsr', swapped, rcv_five, preferred_element_type...]
    pallas_call x0 -> x2, Pallas kernels: none -> 56.2 us  [the longest x1 53.4 us: panels(): pl.pallas_call(panels_kernel, out_shape=(jax.ShapeDtypeStruct(msg_s, bf),...]
    convert_element_type x48 -> x0, other arithmetic: 34.9 us -> none  [the longest x16 20.1 us: source_slant(): sin_b = rcv_sin.astype(jnp.bfloat16)]
    neg x32 -> x0, other arithmetic: 26.1 us -> none  [the longest x16 17 us: source_slant(): bottom = jnp.concatenate([-sin_b, cos_b], axis=2)]
    dynamic_update_slice x32 -> x0, other arithmetic: 25.1 us -> none  [the longest x16 13.4 us: inner(): other = lax.dynamic_update_slice_in_dim(totals[1], rcv_part, offset, 2)]
    another operation x16 -> x0, other arithmetic: 20.8 us -> none  [receiver_outer(): return jnp.transpose(jnp.stack([panel_re, panel_im]), (2, 0, 1, 3))]
  transfers between devices with their start and end apart: 4 -> 0, of which waited for: 4 -> 0; matrix products, arithmetic and copies ran while one was open for 2% -> 0% of each run, Pallas kernels for 0% -> 0%
where the time goes in v2:
time: 62.2 us; the launch traced here: 62 us
  Pallas kernels  56.2 us (90%)
  local copies, waits for them, and re-layouts  5.14 us (8%)
  between operations  0.66 us (1%)
    pallas_call x1, Pallas kernels, panels(): pl.pallas_call(panels_kernel, out_shape=(jax.ShapeDtypeStruct(msg_s, bf),...  53.4 us
    pallas_call x1, Pallas kernels, arrange(): pl.pallas_call(arrange_kernel, out_shape=jax.ShapeDtypeStruct((512, N_FRE...  2.81 us
    transpose x1, local copies, waits for them, and re-layouts, per_device(): src_rows = jnp.transpose(src_spec, (2, 1, 0, 3)).reshape(SB, 16, 128)  1.58 us

profile of v2, /device:TPU:1, one launch (start us, length us, event | category | flops | bytes accessed | tf_op | source)
XLA Modules:
  0.0 62.0 jit_solution(9229006840003537226)
XLA Ops:
  0.6 1.6 %copy.7 = bf16[64,16,2,64]{3,2,1,0:T(2,128)(2,1)S(1)} copy(bf16[64,16,2,64]{3,0,1,2:T(8,128)(2,1)} %bitcast.10) | data formatting | bytes 524288 | tf_op jit(solution)/shard_map/transpose | solution.py:409
  2.2 0.0 copy-start.1
  2.2 1.0 %reshape.16.s_ref = bf16[64,16,128]{2,1,0:T(8,128)(2,1)} reshape(bf16[64,16,2,64]{3,2,1,0:T(2,128)(2,1)S(1)} %copy.7) | data formatting | bytes 524288 | tf_op jit(solution)/shard_map/reshape | solution.py:409
  3.2 0.0 copy-done.1
  3.2 0.6 %copy.8 = bf16[4,2,16,256]{3,2,1,0:T(8,128)(2,1)} copy(bf16[4,2,16,256]{3,0,2,1:T(4,128)(2,1)S(1)} %bitcast.14) | data formatting | bytes 131072 | tf_op jit(solution)/shard_map/transpose | solution.py:410
  3.8 0.0 copy-start.2
  3.8 0.0 copy-start.3
  3.8 0.7 %copy-done.2 = s32[256]{0:T(256)S(1)} copy-done((s32[256]{0:T(256)S(1)}, s32[256]{0:T(256)}, u32[]{:S(2)}) %copy-start.2) | copy-done | bytes 1048
  4.5 0.0 copy-done.3
  4.5 0.6 broadcast_in_dim.3.pos_ref
  5.1 53.4 %panels.1 = (bf16[256,4,128]{2,1,0:T(4,128)(2,1)}, bf16[4,32,256]{2,1,0:T(8,128)(2,1)}) custom-call(bf16[64,16,128]{2,1,0:T(8,128)(2,1)} %reshape.16.s_ref, bf16[4,32,256]{2,1,0:T(8,128)(2,1)} %bitcast.11, s32[16,8192]{1,0:T(8,128)} %table_ref.1, s32[1,320]{1,0:T(1,128)} %broadcast_in_dim.3.pos_ref), custom_call_target="tpu_custom_call" | custom-call | tf_op jit(solution)/shard_map/panels/pallas_call | solution.py:355
  58.5 0.0 copy-start
  58.5 2.8 %arrange.1 = f32[512,256]{1,0:T(8,128)} custom-call(bf16[256,4,128]{2,1,0:T(4,128)(2,1)} %get-tuple-element.4.m_ref), custom_call_target="tpu_custom_call" | custom-call | tf_op jit(solution)/shard_map/arrange/pallas_call | solution.py:400
  61.3 0.0 copy-done
  61.3 0.7 %copy.11 = f32[4,2,16,256]{3,0,1,2:T(4,128)} copy(bf16[4,2,16,256]{3,2,1,0:T(8,128)(2,1)S(1)} %bitcast.13) | data formatting | bytes 196608 | tf_op jit(solution)/shard_map/convert_element_type | solution.py:414
  (1 shorter events, 0.0 us)
Async XLA Ops:
  2.2 1.0 %copy-start.1 = (bf16[2,16,4,256]{3,2,1,0:T(4,128)(2,1)S(1)}, bf16[2,16,4,256]{3,2,1,0:T(4,128)(2,1)}, u32[]{:S(2)}) copy-start(bf16[2,16,4,256]{3,2,1,0:T(4,128)(2,1)} %param.6) | copy-start | bytes 196612
  3.8 0.7 %copy-start.2 = (s32[256]{0:T(256)S(1)}, s32[256]{0:T(256)}, u32[]{:S(2)}) copy-start(s32[256]{0:T(256)} %param.9) | copy-start | bytes 3076
  3.8 0.7 %copy-start.3 = (s32[64]{0:T(128)S(1)}, s32[64]{0:T(128)}, u32[]{:S(2)}) copy-start(s32[64]{0:T(128)} %param.8) | copy-start | bytes 772
  58.5 2.8 %copy-start = (bf16[4,32,256]{2,1,0:T(8,128)(2,1)S(1)}, bf16[4,32,256]{2,1,0:T(8,128)(2,1)}, u32[]{:S(2)}) copy-start(bf16[4,32,256]{2,1,0:T(8,128)(2,1)} %get-tuple-element.5) | copy-start | bytes 196612
